TPU v7x, 32 devices: a whole 2x2x4 slice. The times are simulated.
32 devices in a mesh: groups: 2 (over y), tx: 16 (over z, x, core).
Axes of the slice: x: 2, y: 2, z: 4, core: 2. Of those that a mesh axis runs over, the one named last changes fastest.
Arguments:
- mask: bfloat16 [8192, 1024], P(('groups', 'tx')), parts along dimension 0, may hold values from -1 to 1
- kernel_spectra: float32 [2, 96, 12, 128], replicated, may hold values from -3 to 3
- kernel_weights: float32 [12], replicated, may hold values from 0.1 to 1
- threshold: float32 [1], replicated, may hold values from 0.4 to 1.2
- eval_tile: int32 [16384], P(('groups', 'tx')), parts along dimension 0, may hold values from 0 to 15, as said below
- site_coords: float32 [2, 16, 16384], P(None, None, ('groups', 'tx')), parts along dimension 2, may hold values from 0 to 1
- bias_steps: int32 [16384], P(('groups', 'tx')), parts along dimension 0, may hold values from -4 to 4
Outputs:
- resist: float32 [8192, 1024], P(('groups', 'tx')), parts along dimension 0
- new_bias: float32 [16384], P(('groups', 'tx')), parts along dimension 0
There are 2 independent parts, one for each index of `groups`. A program takes and returns all parts, laid end to end along the dimension named above; an argument that names none is the same for every part. Nothing has to cross between parts.
Inputs may be any that keep to these rules, and one draw needn't show every extreme that they name: `eval_tile`: the evaluating tile of a fragment owned by tile t is t - 1, t or t + 1. One owning tile sends at most 256 fragments to each evaluating tile and exactly 256 to at least one of them; in every draw some tile receives exactly 256 fragments from each of the three owners beside it or itself.
All inputs are finite; a program needn't handle non-finite values.
Results may differ from a plain program's by a relative error of at most 0.0019.
Values may be sent and summed in bfloat16 or wider, within the bound.
A program may use at most 64 MiB of HBM per device.

v0:
```python
import math

import jax
import jax.numpy as jnp
from jax import lax
from jax.sharding import PartitionSpec as P

HALO = 256
BLUR_REACH = 8
SITES = 16


blur_sigma = 3.0
bias_step = 0.5
bias_gain = 2.0


def padded(block, sides, width):
    for axis, dim in sides:
        count = lax.axis_size(axis)
        forward = [(i, i + 1) for i in range(count - 1)]
        backward = [(target, source) for source, target in forward]
        low = lax.ppermute(
            lax.slice_in_dim(block, block.shape[dim] - width, None, axis=dim), axis, forward
        )
        high = lax.ppermute(lax.slice_in_dim(block, 0, width, axis=dim), axis, backward)
        block = jnp.concatenate([low, block, high], axis=dim)
    return block


def twiddle(position, frequency, period, amplitude):
    phase_index = position[:, None] * frequency[None, :] % period
    phase_angle = phase_index.astype(jnp.float32) * (2.0 * math.pi / period)
    return (jnp.cos(phase_angle) * amplitude, jnp.sin(phase_angle) * amplitude)


def centered(count):
    return jnp.arange(count, dtype=jnp.int32) - count // 2


def imaging_tables(tile_rows, tile_cols, window_rows, row_freqs, col_freqs, halo_rows):
    col_cos, col_sin = twiddle(
        jnp.arange(tile_cols, dtype=jnp.int32),
        centered(col_freqs),
        tile_cols,
        1.0 / math.sqrt(tile_cols),
    )
    col_forward = jnp.concatenate([col_cos, -col_sin], axis=1).astype(jnp.bfloat16)
    row_cos, row_sin = twiddle(
        centered(row_freqs),
        jnp.arange(window_rows, dtype=jnp.int32),
        window_rows,
        1.0 / math.sqrt(window_rows),
    )
    row_forward = jnp.concatenate([row_cos, -row_sin], axis=0).astype(jnp.bfloat16)
    back_cos, back_sin = twiddle(
        jnp.arange(tile_rows, dtype=jnp.int32) + halo_rows,
        centered(row_freqs),
        window_rows,
        1.0 / math.sqrt(row_freqs),
    )
    row_inverse = jnp.concatenate([back_cos, back_sin], axis=0).astype(jnp.bfloat16)
    out_cos, out_sin = twiddle(
        centered(col_freqs),
        jnp.arange(tile_cols, dtype=jnp.int32),
        tile_cols,
        1.0 / math.sqrt(col_freqs),
    )
    upper_half = jnp.concatenate([out_cos, out_sin], axis=1)
    lower_half = jnp.concatenate([-out_sin, out_cos], axis=1)
    col_inverse = jnp.concatenate([upper_half, lower_half], axis=0).astype(jnp.bfloat16)
    return (col_forward, row_forward, row_inverse, col_inverse)


def tile_intensity(col_spectra, tables, kernel_spectra, kernel_weights):
    row_forward = tables[1]
    row_inverse = tables[2]
    col_inverse = tables[3]
    row_freqs = kernel_spectra.shape[1]
    kernel_count = kernel_spectra.shape[2]
    col_freqs = kernel_spectra.shape[3]
    tile_rows = row_inverse.shape[0] // 2
    tile_cols = col_inverse.shape[1] // 2
    row_product = jnp.dot(row_forward, col_spectra, preferred_element_type=jnp.float32)
    spec_real = row_product[:row_freqs, :col_freqs] - row_product[row_freqs:, col_freqs:]
    spec_imag = row_product[:row_freqs, col_freqs:] + row_product[row_freqs:, :col_freqs]
    kern_real = kernel_spectra[0]
    kern_imag = kernel_spectra[1]
    prod_real = (kern_real * spec_real[:, None, :] - kern_imag * spec_imag[:, None, :]).astype(
        jnp.bfloat16
    )
    prod_imag = (kern_real * spec_imag[:, None, :] + kern_imag * spec_real[:, None, :]).astype(
        jnp.bfloat16
    )
    flat_width = kernel_count * col_freqs
    joined = jnp.concatenate(
        [prod_real.reshape(row_freqs, flat_width), prod_imag.reshape(row_freqs, flat_width)], axis=1
    )
    back_product = jnp.dot(row_inverse, joined, preferred_element_type=jnp.float32)
    half_real = (
        back_product[:tile_rows, :flat_width] - back_product[tile_rows:, flat_width:]
    ).astype(jnp.bfloat16)
    half_imag = (
        back_product[:tile_rows, flat_width:] + back_product[tile_rows:, :flat_width]
    ).astype(jnp.bfloat16)
    stacked = jnp.concatenate(
        [
            half_real.reshape(tile_rows, kernel_count, col_freqs),
            half_imag.reshape(tile_rows, kernel_count, col_freqs),
        ],
        axis=2,
    )
    stacked = jnp.transpose(stacked, (1, 0, 2))

    def add_kernel(intensity_sum, inputs):
        kernel_block, kernel_weight = inputs
        field_pair = jnp.dot(kernel_block, col_inverse, preferred_element_type=jnp.float32)
        field_real = field_pair[:, :tile_cols]
        field_imag = field_pair[:, tile_cols:]
        return (
            intensity_sum + kernel_weight * (field_real * field_real + field_imag * field_imag),
            None,
        )

    start_sum = jnp.zeros((tile_rows, tile_cols), jnp.float32)
    intensity_sum, unused_out = lax.scan(add_kernel, start_sum, (stacked, kernel_weights))
    return intensity_sum.astype(jnp.bfloat16)


def blur_weight(offset, reach):
    offset_value = offset.astype(jnp.float32)
    all_offsets = jnp.arange(-reach, reach + 1, dtype=jnp.int32).astype(jnp.float32)
    norm_sum = jnp.sum(jnp.exp(-all_offsets * all_offsets / (2.0 * blur_sigma * blur_sigma)))
    inside = jnp.abs(offset) <= reach
    return jnp.where(
        inside,
        jnp.exp(-offset_value * offset_value / (2.0 * blur_sigma * blur_sigma)) / norm_sum,
        jnp.float32(0.0),
    )


def blur_tables(tile_rows, tile_cols, reach):
    col_diff = (
        jnp.arange(tile_cols, dtype=jnp.int32)[None, :]
        - jnp.arange(tile_cols, dtype=jnp.int32)[:, None]
    )
    col_blur = blur_weight(col_diff, reach).astype(jnp.bfloat16)
    row_diff = (
        jnp.arange(tile_rows + 2 * reach, dtype=jnp.int32)[None, :]
        - reach
        - jnp.arange(tile_rows, dtype=jnp.int32)[:, None]
    )
    row_blur = blur_weight(row_diff, reach).astype(jnp.bfloat16)
    return (col_blur, row_blur)


def interp_weights(frac, extent):
    position = frac * (extent - 1)
    low_index = jnp.minimum(jnp.floor(position), extent - 2)
    part = position - low_index
    grid_line = jnp.arange(extent, dtype=jnp.int32).astype(jnp.float32)
    low_hit = (grid_line[None, :] == low_index[:, None]).astype(jnp.float32)
    high_hit = (grid_line[None, :] == low_index[:, None] + 1.0).astype(jnp.float32)
    return low_hit * (1.0 - part)[:, None] + high_hit * part[:, None]


def sample_block(resist, row_frac, col_frac):
    tile_rows, tile_cols = resist.shape
    row_weight = interp_weights(row_frac, tile_rows)
    col_weight = interp_weights(col_frac, tile_cols)
    picked = jnp.dot(
        row_weight, resist, preferred_element_type=jnp.float32, precision=lax.Precision.HIGHEST
    )
    return jnp.sum(picked * col_weight, axis=1)


def slot_ranks(target, target_count):
    frag_count = target.shape[0]
    member = (target[None, :] == jnp.arange(target_count, dtype=jnp.int32)[:, None]).astype(
        jnp.float32
    )
    line = jnp.arange(frag_count, dtype=jnp.int32)
    upper = (line[:, None] <= line[None, :]).astype(jnp.float32)
    inclusive = jnp.dot(
        member, upper, preferred_element_type=jnp.float32, precision=lax.Precision.HIGHEST
    )
    return jnp.sum(member * (inclusive - 1.0), axis=0).astype(jnp.int32)


def shards(mask, kernel_spectra, kernel_weights, threshold, eval_tile, site_coords, bias_steps):
    tile_rows, tile_cols = mask.shape
    window_rows = tile_rows + 2 * HALO
    row_freqs = kernel_spectra.shape[1]
    col_freqs = kernel_spectra.shape[3]
    tables = imaging_tables(tile_rows, tile_cols, window_rows, row_freqs, col_freqs, HALO)
    window = padded(mask, (("tx", 0),), HALO)
    col_spectra = jnp.dot(window, tables[0], preferred_element_type=jnp.float32).astype(
        jnp.bfloat16
    )
    intensity = tile_intensity(col_spectra, tables, kernel_spectra, kernel_weights)
    col_blur, row_blur = blur_tables(tile_rows, tile_cols, BLUR_REACH)
    extended = padded(intensity, (("tx", 0),), BLUR_REACH)
    col_blurred = jnp.dot(extended, col_blur, preferred_element_type=jnp.float32).astype(
        jnp.bfloat16
    )
    resist = jnp.dot(row_blur, col_blurred, preferred_element_type=jnp.float32)
    frag_count = eval_tile.shape[0]
    capacity = frag_count // 2
    records = site_coords.reshape(2 * SITES, frag_count)
    offset_index = eval_tile - lax.axis_index("tx") + 1
    slot_rank = slot_ranks(offset_index, 3)
    target_slot = offset_index * capacity + slot_rank
    slot_line = jnp.arange(3 * capacity, dtype=jnp.int32)
    selector = (target_slot[:, None] == slot_line[None, :]).astype(jnp.float32)
    packed = jnp.dot(
        records, selector, preferred_element_type=jnp.float32, precision=lax.Precision.HIGHEST
    )
    buffer = jnp.transpose(packed.reshape(2 * SITES, 3, capacity), (1, 0, 2))
    arrived = padded(buffer, (("tx", 0),), 1)
    arrived_blocks = arrived[0::2]
    block_means = []
    for block_number in range(3):
        block = arrived_blocks[block_number]
        values = sample_block(resist, block[:SITES].reshape(-1), block[SITES:].reshape(-1))
        block_means.append(jnp.mean(values.reshape(SITES, capacity), axis=0))
    site_means = jnp.stack(block_means, axis=0)
    returned = padded(site_means, (("tx", 0),), 1)[0::2]
    site_mean = jnp.sum(selector * returned.reshape(-1)[None, :], axis=1)
    new_bias = bias_step * bias_steps.astype(jnp.float32) - bias_gain * (site_mean - threshold[0])
    return (resist, new_bias)


def solution(mesh):
    placed = (
        P(("groups", "tx"), None),
        P(),
        P(),
        P(),
        P(("groups", "tx")),
        P(None, None, ("groups", "tx")),
        P(("groups", "tx")),
    )
    return jax.shard_map(
        shards,
        mesh=mesh,
        in_specs=placed,
        out_specs=(P(("groups", "tx"), None), P(("groups", "tx"))),
        check_vma=False,
    )
```

profile of v0, /device:TPU:24, one launch (start us, length us, event | category | flops | bytes accessed | tf_op | source)
XLA Modules:
  0.0 174.5 jit_solution(9952004148682430072)
XLA Ops:
  0.6 2.1 %collective-permute-start = (bf16[256,1024]{1,0:T(8,128)(2,1)}, bf16[256,1024]{1,0:T(8,128)(2,1)}, u32[]{:S(2)}, u32[]{:S(2)}) collective-permute-start(bf16[256,1024]{1,0:T(8,128)(2,1)} %param.9), channel_id=1, source_target_pairs={{0,1},{1,2},{2,3},{3,4},{4,5},{5,6},{6,7},{7,8},{8,9},{9,10},{10,1... | collective-permute-start | bytes 1572872 | tf_op jit(solution)/shard_map/ppermute | solution.py:23
  2.7 4.5 %collective-permute-start.1 = (bf16[256,1024]{1,0:T(8,128)(2,1)}, bf16[256,1024]{1,0:T(8,128)(2,1)}, u32[]{:S(2)}, u32[]{:S(2)}) collective-permute-start(bf16[256,1024]{1,0:T(8,128)(2,1)} %param.9), channel_id=1, source_target_pairs={{1,0},{2,1},{3,2},{4,3},{5,4},{6,5},{7,6},{8,7},{9,8},{10,9},{11,1... | collective-permute-start | bytes 1572872 | tf_op jit(solution)/shard_map/ppermute | solution.py:26
  10.8 1.9 %collective-permute-start.4 = (f32[1,32,256]{2,0,1:T(1,128)}, f32[1,32,256]{2,0,1:T(1,128)}, u32[]{:S(2)}, u32[]{:S(2)}) collective-permute-start(f32[1,32,256]{2,0,1:T(1,128)} %get-tuple-element.84), channel_id=1, source_target_pairs={{0,1},{1,2},{2,3},{3,4},{4,5},{5,6},{6,7},{7,8},{8,9},{9,10},{10,1... | collective-permute-start | bytes 98312 | tf_op jit(solution)/shard_map/ppermute | solution.py:23
  12.7 4.5 %collective-permute-start.5 = (f32[1,32,256]{2,0,1:T(1,128)}, f32[1,32,256]{2,0,1:T(1,128)}, u32[]{:S(2)}, u32[]{:S(2)}) collective-permute-start(f32[1,32,256]{2,0,1:T(1,128)} %get-tuple-element.85), channel_id=1, source_target_pairs={{1,0},{2,1},{3,2},{4,3},{5,4},{6,5},{7,6},{8,7},{9,8},{10,9},{11,1... | collective-permute-start | bytes 98312 | tf_op jit(solution)/shard_map/ppermute | solution.py:26
  17.3 3.0 %multiply_convert_fusion.1 = (bf16[1024,128]{1,0:T(8,128)(2,1)}, bf16[1024,128]{1,0:T(8,128)(2,1)}) fusion(s32[128]{0:T(128)S(1)} %iota_add_fusion.2), kind=kLoop, calls=%fused_computation.121 | loop fusion | flops 2490368 | bytes 524800 | tf_op jit(solution)/shard_map/convert.6
  20.3 2.5 %fusion.112 = (bf16[128,1024]{1,0:T(8,128)(2,1)S(1)}, bf16[128,1024]{1,0:T(8,128)(2,1)S(1)}, bf16[128,1024]{1,0:T(8,128)(2,1)S(1)}) fusion(s32[128]{0:T(128)S(1)} %iota_add_fusion.2), kind=kLoop, calls=%fused_computation.126 | loop fusion | flops 2621440 | bytes 786944 | tf_op jit(solution)/shard_map/convert.5
  24.0 2.1 %multiply_convert_fusion.2 = (bf16[96,768]{1,0:T(8,128)(2,1)}, bf16[96,768]{1,0:T(8,128)(2,1)}) fusion(s32[96]{0:T(128)S(1)} %iota_add_fusion.3), kind=kLoop, calls=%fused_computation.140 | loop fusion | flops 1032192 | bytes 295296 | tf_op jit(solution)/shard_map/convert.8
  26.0 1.3 fusion.164
  34.2 2.5 %fusion.70 = f32[192,256]{1,0:T(8,128)S(1)} fusion(bf16[256,1024]{1,0:T(8,128)(2,1)} %collective-permute-done.1, bf16[256,1024]{1,0:T(8,128)(2,1)} %param.9, bf16[256,1024]{1,0:T(8,128)(2,1)} %collective-permute-done, bf16[1024,128]{1,0:T(8,128)(2,1)} %get-tuple-element.118, bf16[1024,128]{1,0:T(8,128)(2,1)} %get-tuple-element.117, ...), kind=kOutput, calls=%fused_computation.74 | convolution fusion | flops 484704256 | bytes 2588672 | tf_op jit(solution)/shard_map/dot_general | solution.py:84
  41.2 52.7 %while.11 = (s32[]{:T(128)}, f32[256,1024]{1,0:T(8,128)S(1)}, f32[12]{0:T(128)}, bf16[12,256,256]{1,2,0:T(8,128)(2,1)}, bf16[256,2048]{1,0:T(8,128)(2,1)}, /*index=5*/s32[]{:T(128)}, s32[]{:T(128)}) while((s32[]{:T(128)}, f32[256,1024]{1,0:T(8,128)S(1)}, f32[12]{0:T(128)}, bf16[12,256,256]{1,2,0:T(8,128)(2,1)}, ...), condition=%wide.region_2.3_spmd.clone, body=%wide.region_1.2_spmd.clone.sunk | while | flops 270008320 | bytes 7471719 | solution.py:126
  41.2 1.8 %fusion.178 = f32[256,2048]{1,0:T(8,128)S(1)} fusion(bf16[256,2048]{1,0:T(8,128)(2,1)} %get-tuple-element.180, bf16[12,256,256]{1,2,0:T(8,128)(2,1)} %get-tuple-element.179, s32[]{:T(128)} %get-tuple-element.169), kind=kOutput, calls=%fused_computation.5.clone.1 | convolution fusion | flops 268435456 | bytes 3277312 | tf_op jit(solution)/shard_map/while/body/eval_jaxpr/dot_general | solution.py:117
  43.0 1.3 dynamic_slice.17
  44.3 1.3 fusion.179
  45.6 1.8 %fusion.178 = f32[256,2048]{1,0:T(8,128)S(1)} fusion(bf16[256,2048]{1,0:T(8,128)(2,1)} %get-tuple-element.180, bf16[12,256,256]{1,2,0:T(8,128)(2,1)} %get-tuple-element.179, s32[]{:T(128)} %get-tuple-element.169), kind=kOutput, calls=%fused_computation.5.clone.1 | convolution fusion | flops 268435456 | bytes 3277312 | tf_op jit(solution)/shard_map/while/body/eval_jaxpr/dot_general | solution.py:117
  47.4 1.3 dynamic_slice.17
  48.7 1.3 fusion.179
  50.0 1.8 %fusion.178 = f32[256,2048]{1,0:T(8,128)S(1)} fusion(bf16[256,2048]{1,0:T(8,128)(2,1)} %get-tuple-element.180, bf16[12,256,256]{1,2,0:T(8,128)(2,1)} %get-tuple-element.179, s32[]{:T(128)} %get-tuple-element.169), kind=kOutput, calls=%fused_computation.5.clone.1 | convolution fusion | flops 268435456 | bytes 3277312 | tf_op jit(solution)/shard_map/while/body/eval_jaxpr/dot_general | solution.py:117
  51.8 1.3 dynamic_slice.17
  53.1 1.3 fusion.179
  54.4 1.8 %fusion.178 = f32[256,2048]{1,0:T(8,128)S(1)} fusion(bf16[256,2048]{1,0:T(8,128)(2,1)} %get-tuple-element.180, bf16[12,256,256]{1,2,0:T(8,128)(2,1)} %get-tuple-element.179, s32[]{:T(128)} %get-tuple-element.169), kind=kOutput, calls=%fused_computation.5.clone.1 | convolution fusion | flops 268435456 | bytes 3277312 | tf_op jit(solution)/shard_map/while/body/eval_jaxpr/dot_general | solution.py:117
  56.1 1.3 dynamic_slice.17
  57.5 1.3 fusion.179
  58.8 1.8 %fusion.178 = f32[256,2048]{1,0:T(8,128)S(1)} fusion(bf16[256,2048]{1,0:T(8,128)(2,1)} %get-tuple-element.180, bf16[12,256,256]{1,2,0:T(8,128)(2,1)} %get-tuple-element.179, s32[]{:T(128)} %get-tuple-element.169), kind=kOutput, calls=%fused_computation.5.clone.1 | convolution fusion | flops 268435456 | bytes 3277312 | tf_op jit(solution)/shard_map/while/body/eval_jaxpr/dot_general | solution.py:117
  60.5 1.3 dynamic_slice.17
  61.9 1.3 fusion.179
  63.2 1.8 %fusion.178 = f32[256,2048]{1,0:T(8,128)S(1)} fusion(bf16[256,2048]{1,0:T(8,128)(2,1)} %get-tuple-element.180, bf16[12,256,256]{1,2,0:T(8,128)(2,1)} %get-tuple-element.179, s32[]{:T(128)} %get-tuple-element.169), kind=kOutput, calls=%fused_computation.5.clone.1 | convolution fusion | flops 268435456 | bytes 3277312 | tf_op jit(solution)/shard_map/while/body/eval_jaxpr/dot_general | solution.py:117
  64.9 1.3 dynamic_slice.17
  67.5 1.8 %fusion.178 = f32[256,2048]{1,0:T(8,128)S(1)} fusion(bf16[256,2048]{1,0:T(8,128)(2,1)} %get-tuple-element.180, bf16[12,256,256]{1,2,0:T(8,128)(2,1)} %get-tuple-element.179, s32[]{:T(128)} %get-tuple-element.169), kind=kOutput, calls=%fused_computation.5.clone.1 | convolution fusion | flops 268435456 | bytes 3277312 | tf_op jit(solution)/shard_map/while/body/eval_jaxpr/dot_general | solution.py:117
  69.3 1.3 dynamic_slice.17
  71.9 1.8 %fusion.178 = f32[256,2048]{1,0:T(8,128)S(1)} fusion(bf16[256,2048]{1,0:T(8,128)(2,1)} %get-tuple-element.180, bf16[12,256,256]{1,2,0:T(8,128)(2,1)} %get-tuple-element.179, s32[]{:T(128)} %get-tuple-element.169), kind=kOutput, calls=%fused_computation.5.clone.1 | convolution fusion | flops 268435456 | bytes 3277312 | tf_op jit(solution)/shard_map/while/body/eval_jaxpr/dot_general | solution.py:117
  73.7 1.3 dynamic_slice.17
  76.3 1.8 %fusion.178 = f32[256,2048]{1,0:T(8,128)S(1)} fusion(bf16[256,2048]{1,0:T(8,128)(2,1)} %get-tuple-element.180, bf16[12,256,256]{1,2,0:T(8,128)(2,1)} %get-tuple-element.179, s32[]{:T(128)} %get-tuple-element.169), kind=kOutput, calls=%fused_computation.5.clone.1 | convolution fusion | flops 268435456 | bytes 3277312 | tf_op jit(solution)/shard_map/while/body/eval_jaxpr/dot_general | solution.py:117
  78.1 1.3 dynamic_slice.17
  80.7 1.8 %fusion.178 = f32[256,2048]{1,0:T(8,128)S(1)} fusion(bf16[256,2048]{1,0:T(8,128)(2,1)} %get-tuple-element.180, bf16[12,256,256]{1,2,0:T(8,128)(2,1)} %get-tuple-element.179, s32[]{:T(128)} %get-tuple-element.169), kind=kOutput, calls=%fused_computation.5.clone.1 | convolution fusion | flops 268435456 | bytes 3277312 | tf_op jit(solution)/shard_map/while/body/eval_jaxpr/dot_general | solution.py:117
  82.5 1.3 dynamic_slice.17
  85.1 1.8 %fusion.178 = f32[256,2048]{1,0:T(8,128)S(1)} fusion(bf16[256,2048]{1,0:T(8,128)(2,1)} %get-tuple-element.180, bf16[12,256,256]{1,2,0:T(8,128)(2,1)} %get-tuple-element.179, s32[]{:T(128)} %get-tuple-element.169), kind=kOutput, calls=%fused_computation.5.clone.1 | convolution fusion | flops 268435456 | bytes 3277312 | tf_op jit(solution)/shard_map/while/body/eval_jaxpr/dot_general | solution.py:117
  86.9 1.3 dynamic_slice.17
  89.5 1.8 %fusion.178 = f32[256,2048]{1,0:T(8,128)S(1)} fusion(bf16[256,2048]{1,0:T(8,128)(2,1)} %get-tuple-element.180, bf16[12,256,256]{1,2,0:T(8,128)(2,1)} %get-tuple-element.179, s32[]{:T(128)} %get-tuple-element.169), kind=kOutput, calls=%fused_computation.5.clone.1 | convolution fusion | flops 268435456 | bytes 3277312 | tf_op jit(solution)/shard_map/while/body/eval_jaxpr/dot_general | solution.py:117
  91.3 1.3 dynamic_slice.17
  94.0 1.9 %collective-permute-start.2 = (bf16[8,1024]{1,0:T(8,128)(2,1)S(1)}, bf16[8,1024]{1,0:T(8,128)(2,1)S(1)}, u32[]{:S(2)}, u32[]{:S(2)}) collective-permute-start(bf16[8,1024]{1,0:T(8,128)(2,1)S(1)} %get-tuple-element.74), channel_id=1, source_target_pairs={{0,1},{1,2},{2,3},{3,4},{4,5},{5,6},{6,7},{7,8},{8,9},{9,10},{10,1... | collective-permute-start | bytes 49160 | tf_op jit(solution)/shard_map/ppermute | solution.py:23
  95.9 4.7 %collective-permute-start.3 = (bf16[8,1024]{1,0:T(8,128)(2,1)S(1)}, bf16[8,1024]{1,0:T(8,128)(2,1)S(1)}, u32[]{:S(2)}, u32[]{:S(2)}) collective-permute-start(bf16[8,1024]{1,0:T(8,128)(2,1)S(1)} %get-tuple-element.75), channel_id=1, source_target_pairs={{1,0},{2,1},{3,2},{4,3},{5,4},{6,5},{7,6},{8,7},{9,8},{10,9},{11,1... | collective-permute-start | bytes 49160 | tf_op jit(solution)/shard_map/ppermute | solution.py:26
  101.9 1.6 fusion.64
  103.7 19.7 %multiply_reduce_fusion = f32[4096]{0:T(1024)S(1)} fusion(f32[256,1024]{1,0:T(8,128)S(1)} %fusion.64, f32[4096]{0:T(1024)S(1)} %copy-done.9, f32[4096]{0:T(1024)S(1)} %copy-done.8, f32[4096]{0:T(1024)S(1)} %copy-done.7, f32[4096]{0:T(1024)S(1)} %copy-done.6, f32[1024]{0:T(1024)S(1)} %copy-done.16, f32[4096]{0:T(1024)S(1)} %copy-done.10, ...), kind=kOutput, calls=%fused_computation.9 | convolution fusion | flops 12919500800 | bytes 1201152 | tf_op jit(solution)/shard_map/dot_general | solution.py:171
  123.4 19.7 %multiply_reduce_fusion.1 = f32[4096]{0:T(1024)S(1)} fusion(f32[256,1024]{1,0:T(8,128)S(1)} %fusion.64, f32[4096]{0:T(1024)S(1)} %copy-done.1, f32[4096]{0:T(1024)S(1)} %get-tuple-element.100, f32[4096]{0:T(1024)S(1)} %get-tuple-element.99, f32[4096]{0:T(1024)S(1)} %get-tuple-element.98, f32[1024]{0:T(1024)S(1)} %copy-done.16, f32[4096]{0:T(1024)S(1)} %copy-done.2, ...), kind=kOutput, calls=%fused_computation.10 | convolution fusion | flops 12919500800 | bytes 1201152 | tf_op jit(solution)/shard_map/dot_general | solution.py:171
  143.2 4.7 %collective-permute-start.7 = (f32[1,256]{1,0:T(1,128)S(1)}, f32[1,256]{1,0:T(1,128)S(1)}, u32[]{:S(2)}, u32[]{:S(2)}) collective-permute-start(f32[1,256]{1,0:T(1,128)S(1)} %bitcast.80), channel_id=1, source_target_pairs={{1,0},{2,1},{3,2},{4,3},{5,4},{6,5},{7,6},{8,7},{9,8},{10,9},{11,1... | collective-permute-start | bytes 3080 | tf_op jit(solution)/shard_map/ppermute | solution.py:26
  148.0 19.7 %multiply_reduce_fusion.2 = f32[4096]{0:T(1024)S(1)} fusion(f32[256,1024]{1,0:T(8,128)S(1)} %fusion.64, f32[4096]{0:T(1024)S(1)} %get-tuple-element.109, f32[4096]{0:T(1024)S(1)} %get-tuple-element.108, f32[4096]{0:T(1024)S(1)} %get-tuple-element.107, f32[4096]{0:T(1024)S(1)} %get-tuple-element.106, f32[1024]{0:T(1024)S(1)} %copy-done.16, ...), kind=kOutput, calls=%fused_computation.11 | convolution fusion | flops 12919500800 | bytes 1201152 | tf_op jit(solution)/shard_map/dot_general | solution.py:171
  167.7 1.9 %collective-permute-start.6 = (f32[1,256]{1,0:T(1,128)S(1)}, f32[1,256]{1,0:T(1,128)S(1)}, u32[]{:S(2)}, u32[]{:S(2)}) collective-permute-start(f32[1,256]{1,0:T(1,128)S(1)} %bitcast.82), channel_id=1, source_target_pairs={{0,1},{1,2},{2,3},{3,4},{4,5},{5,6},{6,7},{7,8},{8,9},{9,10},{10,1... | collective-permute-start | bytes 3080 | tf_op jit(solution)/shard_map/ppermute | solution.py:23
  169.7 3.8 %collective-permute-done.6 = f32[1,256]{1,0:T(1,128)S(1)} collective-permute-done((f32[1,256]{1,0:T(1,128)S(1)}, f32[1,256]{1,0:T(1,128)S(1)}, u32[]{:S(2)}, u32[]{:S(2)}) %collective-permute-start.6) | collective-permute-done | bytes 1056 | tf_op jit(solution)/shard_map/ppermute | solution.py:23
  (105 shorter events, 26.7 us)
Async XLA Ops:
  0.6 8.2 %copy-start = (f32[2,16,512]{2,1,0:T(8,128)S(1)}, f32[2,16,512]{2,1,0:T(8,128)}, u32[]{:S(2)}) copy-start(f32[2,16,512]{2,1,0:T(8,128)} %param.14) | copy-start | bytes 196612
  0.6 33.5 %collective-permute-start = (bf16[256,1024]{1,0:T(8,128)(2,1)}, bf16[256,1024]{1,0:T(8,128)(2,1)}, u32[]{:S(2)}, u32[]{:S(2)}) collective-permute-start(bf16[256,1024]{1,0:T(8,128)(2,1)} %param.9), channel_id=1, source_target_pairs={{0,1},{1,2},{2,3},{3,4},{4,5},{5,6},{6,7},{7,8},{8,9},{9,10},{10,1... | collective-permute-start | bytes 1572872 | tf_op jit(solution)/shard_map/ppermute | solution.py:23
  2.7 31.5 %collective-permute-start.1 = (bf16[256,1024]{1,0:T(8,128)(2,1)}, bf16[256,1024]{1,0:T(8,128)(2,1)}, u32[]{:S(2)}, u32[]{:S(2)}) collective-permute-start(bf16[256,1024]{1,0:T(8,128)(2,1)} %param.9), channel_id=1, source_target_pairs={{1,0},{2,1},{3,2},{4,3},{5,4},{6,5},{7,6},{8,7},{9,8},{10,9},{11,1... | collective-permute-start | bytes 1572872 | tf_op jit(solution)/shard_map/ppermute | solution.py:26
  8.8 0.6 copy-start.14
  10.8 20.7 %collective-permute-start.4 = (f32[1,32,256]{2,0,1:T(1,128)}, f32[1,32,256]{2,0,1:T(1,128)}, u32[]{:S(2)}, u32[]{:S(2)}) collective-permute-start(f32[1,32,256]{2,0,1:T(1,128)} %get-tuple-element.84), channel_id=1, source_target_pairs={{0,1},{1,2},{2,3},{3,4},{4,5},{5,6},{6,7},{7,8},{8,9},{9,10},{10,1... | collective-permute-start | bytes 98312 | tf_op jit(solution)/shard_map/ppermute | solution.py:23
  12.7 18.8 %collective-permute-start.5 = (f32[1,32,256]{2,0,1:T(1,128)}, f32[1,32,256]{2,0,1:T(1,128)}, u32[]{:S(2)}, u32[]{:S(2)}) collective-permute-start(f32[1,32,256]{2,0,1:T(1,128)} %get-tuple-element.85), channel_id=1, source_target_pairs={{1,0},{2,1},{3,2},{4,3},{5,4},{6,5},{7,6},{8,7},{9,8},{10,9},{11,1... | collective-permute-start | bytes 98312 | tf_op jit(solution)/shard_map/ppermute | solution.py:26
  41.2 60.7 %copy-start.18 = (s32[272]{0:T(512)S(1)}, s32[272]{0:T(512)}, u32[]{:S(2)}) copy-start(s32[272]{0:T(512)} %iota_add_fusion) | copy-start | bytes 3268
  94.0 6.8 %collective-permute-start.2 = (bf16[8,1024]{1,0:T(8,128)(2,1)S(1)}, bf16[8,1024]{1,0:T(8,128)(2,1)S(1)}, u32[]{:S(2)}, u32[]{:S(2)}) collective-permute-start(bf16[8,1024]{1,0:T(8,128)(2,1)S(1)} %get-tuple-element.74), channel_id=1, source_target_pairs={{0,1},{1,2},{2,3},{3,4},{4,5},{5,6},{6,7},{7,8},{8,9},{9,10},{10,1... | collective-permute-start | bytes 49160 | tf_op jit(solution)/shard_map/ppermute | solution.py:23
  95.9 6.0 %collective-permute-start.3 = (bf16[8,1024]{1,0:T(8,128)(2,1)S(1)}, bf16[8,1024]{1,0:T(8,128)(2,1)S(1)}, u32[]{:S(2)}, u32[]{:S(2)}) collective-permute-start(bf16[8,1024]{1,0:T(8,128)(2,1)S(1)} %get-tuple-element.75), channel_id=1, source_target_pairs={{1,0},{2,1},{3,2},{4,3},{5,4},{6,5},{7,6},{8,7},{9,8},{10,9},{11,1... | collective-permute-start | bytes 49160 | tf_op jit(solution)/shard_map/ppermute | solution.py:26
  100.6 2.9 %copy-start.6 = (f32[4096]{0:T(1024)S(1)}, f32[4096]{0:T(1024)}, u32[]{:S(2)}) copy-start(f32[4096]{0:T(1024)} %get-tuple-element.90) | copy-start | bytes 49156
  100.7 2.9 %copy-start.7 = (f32[4096]{0:T(1024)S(1)}, f32[4096]{0:T(1024)}, u32[]{:S(2)}) copy-start(f32[4096]{0:T(1024)} %get-tuple-element.91) | copy-start | bytes 49156
  100.7 2.9 %copy-start.8 = (f32[4096]{0:T(1024)S(1)}, f32[4096]{0:T(1024)}, u32[]{:S(2)}) copy-start(f32[4096]{0:T(1024)} %get-tuple-element.92) | copy-start | bytes 49156
  100.7 2.9 %copy-start.9 = (f32[4096]{0:T(1024)S(1)}, f32[4096]{0:T(1024)}, u32[]{:S(2)}) copy-start(f32[4096]{0:T(1024)} %get-tuple-element.93) | copy-start | bytes 49156
  100.7 2.9 %copy-start.10 = (f32[4096]{0:T(1024)S(1)}, f32[4096]{0:T(1024)}, u32[]{:S(2)}) copy-start(f32[4096]{0:T(1024)} %get-tuple-element.127) | copy-start | bytes 49156
  100.7 2.9 %copy-start.11 = (f32[4096]{0:T(1024)S(1)}, f32[4096]{0:T(1024)}, u32[]{:S(2)}) copy-start(f32[4096]{0:T(1024)} %get-tuple-element.128) | copy-start | bytes 49156
  100.7 2.9 %copy-start.12 = (f32[4096]{0:T(1024)S(1)}, f32[4096]{0:T(1024)}, u32[]{:S(2)}) copy-start(f32[4096]{0:T(1024)} %get-tuple-element.129) | copy-start | bytes 49156
  100.7 2.9 %copy-start.13 = (f32[4096]{0:T(1024)S(1)}, f32[4096]{0:T(1024)}, u32[]{:S(2)}) copy-start(f32[4096]{0:T(1024)} %get-tuple-element.130) | copy-start | bytes 49156
  100.7 2.9 %copy-start.16 = (f32[1024]{0:T(1024)S(1)}, f32[1024]{0:T(1024)}, u32[]{:S(2)}) copy-start(f32[1024]{0:T(1024)} %iota_convert_fusion) | copy-start | bytes 12292
  100.7 2.9 %copy-start.20 = (f32[256]{0:T(256)S(1)}, f32[256]{0:T(256)}, u32[]{:S(2)}) copy-start(f32[256]{0:T(256)} %iota_convert_fusion.1) | copy-start | bytes 3076
  103.5 44.5 %copy-start.19 = (f32[256,1024]{1,0:T(8,128)}, f32[256,1024]{1,0:T(8,128)S(1)}, u32[]{:S(2)}) copy-start(f32[256,1024]{1,0:T(8,128)S(1)} %fusion.64) | copy-start | bytes 3145732
  103.6 19.8 %copy-start.1 = (f32[4096]{0:T(1024)S(1)}, f32[4096]{0:T(1024)}, u32[]{:S(2)}) copy-start(f32[4096]{0:T(1024)} %get-tuple-element.101) | copy-start | bytes 49156
  103.6 19.8 %copy-start.2 = (f32[4096]{0:T(1024)S(1)}, f32[4096]{0:T(1024)}, u32[]{:S(2)}) copy-start(f32[4096]{0:T(1024)} %get-tuple-element.123) | copy-start | bytes 49156
  103.6 19.8 %copy-start.3 = (f32[4096]{0:T(1024)S(1)}, f32[4096]{0:T(1024)}, u32[]{:S(2)}) copy-start(f32[4096]{0:T(1024)} %get-tuple-element.124) | copy-start | bytes 49156
  103.6 19.8 %copy-start.4 = (f32[4096]{0:T(1024)S(1)}, f32[4096]{0:T(1024)}, u32[]{:S(2)}) copy-start(f32[4096]{0:T(1024)} %get-tuple-element.125) | copy-start | bytes 49156
  103.7 19.8 %copy-start.5 = (f32[4096]{0:T(1024)S(1)}, f32[4096]{0:T(1024)}, u32[]{:S(2)}) copy-start(f32[4096]{0:T(1024)} %get-tuple-element.126) | copy-start | bytes 49156
  143.2 26.5 %collective-permute-start.7 = (f32[1,256]{1,0:T(1,128)S(1)}, f32[1,256]{1,0:T(1,128)S(1)}, u32[]{:S(2)}, u32[]{:S(2)}) collective-permute-start(f32[1,256]{1,0:T(1,128)S(1)} %bitcast.80), channel_id=1, source_target_pairs={{1,0},{2,1},{3,2},{4,3},{5,4},{6,5},{7,6},{8,7},{9,8},{10,9},{11,1... | collective-permute-start | bytes 3080 | tf_op jit(solution)/shard_map/ppermute | solution.py:26
  148.0 25.6 %copy-start.15 = (s32[512]{0:T(512)S(1)}, s32[512]{0:T(512)}, u32[]{:S(2)}) copy-start(s32[512]{0:T(512)} %copy-done.14) | copy-start | bytes 6148
  148.0 25.9 %copy-start.17 = (s32[512]{0:T(512)S(1)}, s32[512]{0:T(512)}, u32[]{:S(2)}) copy-start(s32[512]{0:T(512)} %param.15) | copy-start | bytes 6148
  167.7 5.8 %collective-permute-start.6 = (f32[1,256]{1,0:T(1,128)S(1)}, f32[1,256]{1,0:T(1,128)S(1)}, u32[]{:S(2)}, u32[]{:S(2)}) collective-permute-start(f32[1,256]{1,0:T(1,128)S(1)} %bitcast.82), channel_id=1, source_target_pairs={{0,1},{1,2},{2,3},{3,4},{4,5},{5,6},{6,7},{7,8},{8,9},{9,10},{10,1... | collective-permute-start | bytes 3080 | tf_op jit(solution)/shard_map/ppermute | solution.py:23
where the time goes:
time: 176 us; the launch traced here: 174 us
  matrix products  86.1 us (49%)
  other arithmetic  34.5 us (20%)
  starting transfers between devices  26.4 us (15%)
  local copies, waits for them, and re-layouts  20.3 us (12%)
  waiting for transfers between devices  4.96 us (3%)
  between operations  1.91 us (1%)
    dot_general x3, matrix products, sample_block(): jnp.dot(row_weight, resist, preferred_element_type=jnp.float32, precision...  59.1 us
    dot_general x12, matrix products, add_kernel(): jnp.dot(kernel_block, col_inverse, preferred_element_type=jnp.float32)  21.2 us
    ppermute x4, starting transfers between devices, padded(): lax.ppermute(lax.slice_in_dim(block, 0, width, axis=dim), axis, backward)  18.6 us
    dynamic_slice x12, local copies, waits for them, and re-layouts, tile_intensity(): lax.scan(add_kernel, start_sum, (stacked, kernel_weights))  15.9 us
    add x12, other arithmetic, add_kernel(): intensity_sum + kernel_weight * (field_real * field_real + field_imag * f...  15.4 us
    another operation x4, other arithmetic  8.14 us
    ppermute x4, starting transfers between devices, padded(): lax.ppermute(lax.slice_in_dim(block, block.shape[dim] - width, None, axis...  7.81 us
    ppermute x4, waiting for transfers between devices, padded(): lax.ppermute(lax.slice_in_dim(block, block.shape[dim] - width, None, axis...  3.84 us
  transfers between devices with their start and end apart: 8, of which 2 were waited for; matrix products, arithmetic and copies ran while one was open for 22% of the time, Pallas kernels for 0%

commit v1 on v0

v1 whole, which is shorter than its diff:
```python
import math

import jax
import jax.numpy as jnp
import ml_dtypes
import numpy as np
from jax import lax
from jax.experimental import pallas as pl
from jax.experimental.pallas import tpu as pltpu
from jax.sharding import PartitionSpec as P

HALO = 256
REACH = 8
SITES = 16
GRID_STEP = 4
BLOCK = 64
SIGMA = 3.0
BF = jnp.bfloat16
F32 = jnp.float32
MESH = pl.DeviceIdType.MESH


def host_bf16(x):
    return np.asarray(x, np.float32).astype(ml_dtypes.bfloat16)


def twiddle(position, frequency, period, amplitude):
    index = (position[:, None] * frequency[None, :]) % period
    angle = index.astype(np.float64) * (2.0 * math.pi / period)
    return np.cos(angle) * amplitude, np.sin(angle) * amplitude


def gauss(offset):
    every = np.arange(-REACH, REACH + 1)
    norm = np.sum(np.exp(-every * every / (2.0 * SIGMA * SIGMA)))
    value = np.exp(-offset * offset / (2.0 * SIGMA * SIGMA)) / norm
    return np.where(np.abs(offset) <= REACH, value, 0.0)


def split2(x):
    high = host_bf16(x)
    low = host_bf16(x - high.astype(np.float64))
    return high, low


def tables(rows, cols, row_freqs, col_freqs):
    window = rows + 2 * HALO
    f = np.arange(col_freqs) - col_freqs // 2
    g = np.arange(row_freqs) - row_freqs // 2
    c, s = twiddle(np.arange(cols), f, cols, 1.0 / math.sqrt(cols))
    col_forward = host_bf16(np.concatenate([c, -s], 1))
    c, s = twiddle(g, np.arange(window), window, 1.0 / math.sqrt(window))
    row_forward = host_bf16(np.concatenate([c, -s], 0))
    c, s = twiddle(np.arange(rows) + HALO, g, window, 1.0 / math.sqrt(row_freqs))
    row_inverse = host_bf16(np.block([[c, -s], [s, c]]))
    picked = np.arange(0, cols, GRID_STEP)
    c, s = twiddle(f, picked, cols, 1.0 / math.sqrt(col_freqs))
    col_inverse = host_bf16(np.block([[c, s], [-s, c]]))
    diff = np.arange(cols)[None, :] - picked[:, None]
    order = np.arange(1, col_freqs)
    base = np.arange(cols)
    kernel = 1.0 + 2.0 * np.cos(2 * math.pi * ((base[:, None] * order[None, :]) % cols) / cols).sum(1)
    kernel = (kernel + np.cos(2 * math.pi * ((base * col_freqs) % cols) / cols)) / picked.size
    interp = kernel[diff % cols]
    lines = np.arange(cols)
    col_blur = host_bf16(gauss((lines[None, :] - lines[:, None]).astype(np.float64)))
    spread = interp @ col_blur.astype(np.float64)
    high, low = split2(spread)
    wide = np.concatenate([high, low], 0)
    row_diff = np.arange(rows + 2 * REACH)[None, :] - REACH - np.arange(rows)[:, None]
    row_blur = host_bf16(gauss(row_diff.astype(np.float64)))
    row_mid = np.ascontiguousarray(row_blur[:, REACH:REACH + rows])
    row_edge = np.concatenate([row_blur[:, :REACH], row_blur[:, REACH + rows:]], 1)
    return (col_forward, row_forward, row_inverse, col_inverse, row_mid, row_edge, wide,
            np.ascontiguousarray(high.T))


def dot(a, b):
    return jnp.dot(a, b, preferred_element_type=F32)


def dot_nt(a, b):
    return lax.dot_general(a, b, (((1,), (1,)), ((), ())), preferred_element_type=F32)


def split3(x):
    high = x.astype(BF)
    rest = x - high.astype(F32)
    mid = rest.astype(BF)
    low = (rest - mid.astype(F32)).astype(BF)
    return jnp.concatenate([high, mid, low], axis=0)


def hat(distance):
    return jnp.maximum(1.0 - jnp.abs(distance), 0.0)


def kernel(mask, spectra, weights, thresh, ev, sc, bias, colf, rowf, rinv, cinv, rmid, redge,
           wide_h, wide_t_h, resist_h, nb,
           win, snd, recs, inten, hsnd, halo, rsnd, ret, sel, ksv, wide, wide_t, resist, rt,
           local_sem, send_sem, recv_sem):
    t = lax.axis_index("tx")
    count = lax.axis_size("tx")
    has_left = t > 0
    has_right = t < count - 1
    rows, cols = mask.shape
    row_freqs, kernels, col_freqs = ksv.shape[1:]
    frags = ev.shape[1]
    cap = frags // 2

    barrier = pltpu.get_barrier_semaphore()

    @pl.when(has_left)
    def _():
        pl.semaphore_signal(barrier, inc=1, device_id={"tx": t - 1}, device_id_type=MESH)

    @pl.when(has_right)
    def _():
        pl.semaphore_signal(barrier, inc=1, device_id={"tx": t + 1}, device_id_type=MESH)

    load_ks = pltpu.make_async_copy(spectra, ksv, local_sem.at[0])
    load_wide = pltpu.make_async_copy(wide_h, wide, local_sem.at[1])
    load_wide_t = pltpu.make_async_copy(wide_t_h, wide_t, local_sem.at[2])
    load_ks.start()
    load_wide.start()
    load_wide_t.start()

    def to_left(kind, src, dst):
        return pltpu.make_async_remote_copy(
            src_ref=src, dst_ref=dst, send_sem=send_sem.at[kind, 0], recv_sem=recv_sem.at[kind, 0],
            device_id={"tx": t - 1}, device_id_type=MESH)

    def to_right(kind, src, dst):
        return pltpu.make_async_remote_copy(
            src_ref=src, dst_ref=dst, send_sem=send_sem.at[kind, 1], recv_sem=recv_sem.at[kind, 1],
            device_id={"tx": t + 1}, device_id_type=MESH)

    own = win.at[pl.ds(HALO, rows)]
    pairs = (
        (to_left(0, own, win.at[pl.ds(HALO + rows, HALO)]), to_right(0, own, win.at[pl.ds(0, HALO)])),
        (to_left(1, snd.at[0], recs.at[2]), to_right(1, snd.at[2], recs.at[0])),
        (to_left(2, hsnd.at[0], halo.at[1]), to_right(2, hsnd.at[1], halo.at[0])),
        (to_left(3, rsnd.at[0], ret.at[2]), to_right(3, rsnd.at[2], ret.at[0])),
    )

    def start(kind):
        @pl.when(has_left)
        def _():
            pairs[kind][0].start()

        @pl.when(has_right)
        def _():
            pairs[kind][1].start()

    def arrive(kind):
        @pl.when(has_right)
        def _():
            pairs[kind][0].wait_recv()

        @pl.when(has_left)
        def _():
            pairs[kind][1].wait_recv()

    @pl.when(jnp.logical_not(has_left))
    def _():
        win[0:HALO] = jnp.zeros((HALO, win.shape[1]), BF)
        recs[0] = jnp.zeros(recs.shape[1:], F32)
        halo[0] = jnp.zeros(halo.shape[1:], F32)
        ret[0] = jnp.zeros(ret.shape[1:], F32)

    @pl.when(jnp.logical_not(has_right))
    def _():
        win[HALO + rows:] = jnp.zeros((HALO, win.shape[1]), BF)
        recs[2] = jnp.zeros(recs.shape[1:], F32)
        halo[1] = jnp.zeros(halo.shape[1:], F32)
        ret[2] = jnp.zeros(ret.shape[1:], F32)

    win[HALO:HALO + rows] = dot(mask[...], colf[...]).astype(BF)

    between = jnp.logical_and(has_left, has_right)

    @pl.when(between)
    def _():
        pl.semaphore_wait(barrier, 2)

    @pl.when(jnp.logical_not(between))
    def _():
        pl.semaphore_wait(barrier, 1)

    start(0)

    offset = ev[...] - t + 1
    member = jnp.where(lax.broadcasted_iota(jnp.int32, (8, frags), 0) == offset, 1.0, 0.0)
    upper = jnp.where(
        lax.broadcasted_iota(jnp.int32, (frags, frags), 0)
        <= lax.broadcasted_iota(jnp.int32, (frags, frags), 1), 1.0, 0.0).astype(BF)
    inclusive = dot(member.astype(BF), upper)
    rank = jnp.sum(member * (inclusive - 1.0), axis=0, keepdims=True)
    slot = offset.astype(F32) * float(cap) + rank
    slot_line = lax.broadcasted_iota(jnp.int32, (3 * cap, frags), 0).astype(F32)
    sel[...] = jnp.where(slot_line == slot, 1.0, 0.0).astype(BF)
    records = jnp.concatenate([sc[0], sc[1]], axis=0)
    packed = dot_nt(split3(records), sel[...])
    n_rec = 2 * SITES
    packed = packed[:n_rec] + packed[n_rec:2 * n_rec] + packed[2 * n_rec:]
    snd[0] = packed[:, :cap]
    recs[1] = packed[:, cap:2 * cap]
    snd[2] = packed[:, 2 * cap:]
    start(1)

    product = dot(rowf[:, HALO:HALO + rows], win[HALO:HALO + rows])
    load_ks.wait()
    arrive(0)
    product = product + dot(rowf[:, :HALO], win[:HALO]) + dot(rowf[:, HALO + rows:], win[HALO + rows:])
    real = product[:row_freqs, :col_freqs] - product[row_freqs:, col_freqs:]
    imag = product[:row_freqs, col_freqs:] + product[row_freqs:, :col_freqs]

    total = jnp.zeros((rows, cinv.shape[1] // 2), F32)
    half = cinv.shape[1] // 2
    for pair in range(kernels // 2):
        blocks = []
        for k in (2 * pair, 2 * pair + 1):
            kr = ksv[0, :, k, :]
            ki = ksv[1, :, k, :]
            blocks.append(jnp.concatenate(
                [(kr * real - ki * imag).astype(BF), (kr * imag + ki * real).astype(BF)], axis=0))
        field = dot(rinv[...], jnp.concatenate(blocks, axis=1)).astype(BF)
        for i in range(2):
            part = field[:, i * col_freqs:(i + 1) * col_freqs]
            e = dot(jnp.concatenate([part[:rows], part[rows:]], axis=1), cinv[...])
            er = e[:, :half]
            ei = e[:, half:]
            total = total + weights[2 * pair + i] * (er * er + ei * ei)

    rounded = total.astype(BF)
    inten[...] = rounded
    hsnd[0] = rounded[:REACH].astype(F32)
    hsnd[1] = rounded[rows - REACH:].astype(F32)
    start(2)
    blurred = dot(rmid[...], inten[...])
    arrive(2)
    edge = jnp.concatenate([halo[0], halo[1]], axis=0).astype(BF)
    blurred = blurred + dot(redge[...], edge)
    center = jnp.sum(blurred) * (1.0 / (blurred.shape[0] * blurred.shape[1]))
    high = blurred.astype(BF)
    low = (blurred - high.astype(F32)).astype(BF)
    load_wide_t.wait()
    rt[...] = (dot_nt(wide_t[...], high) + dot_nt(wide_t[...], low) - center).astype(BF)
    load_wide.wait()
    coarse = high.shape[1]
    resist[...] = (dot(high, wide[:coarse]) + dot(low, wide[:coarse])) + dot(high, wide[coarse:])
    store = pltpu.make_async_copy(resist, resist_h, local_sem.at[3])
    store.start()
    arrive(1)

    blocks_n = cols // BLOCK
    row_line = lax.broadcasted_iota(jnp.int32, (rows, cap), 0).astype(F32)
    col_line = lax.broadcasted_iota(jnp.int32, (BLOCK, cap), 0).astype(F32)
    end_line = lax.broadcasted_iota(jnp.int32, (8, cap), 0).astype(F32) + float(BLOCK)

    def evaluate(block):
        def one(s, acc):
            p = recs[block, pl.ds(s, 1), :] * float(rows - 1)
            q = recs[block, pl.ds(SITES + s, 1), :] * float(cols - 1)
            wr = hat(row_line - p).astype(BF)
            lines = dot(rt[...], wr)
            h = jnp.floor(q * (1.0 / BLOCK))
            local = q - h * float(BLOCK)
            chosen = lines[:BLOCK]
            after = jnp.zeros((8, cap), F32)
            for k in range(1, blocks_n):
                here = lines[k * BLOCK:(k + 1) * BLOCK]
                chosen = jnp.where(h == float(k), here, chosen)
                after = jnp.where(h == float(k - 1), here[:8], after)
            weighted = chosen * hat(col_line - local)
            for g in range(BLOCK // 8):
                acc = acc + weighted[g * 8:(g + 1) * 8]
            return acc + after * hat(end_line - local)

        def step(i, acc):
            return one(2 * i + 1, one(2 * i, acc))

        acc = lax.fori_loop(0, SITES // 2, step, jnp.zeros((8, cap), F32))
        mean = jnp.sum(acc, axis=0, keepdims=True) * (1.0 / SITES) + center
        return jnp.broadcast_to(mean, (8, cap))

    rsnd[0] = evaluate(0)
    rsnd[2] = evaluate(2)
    start(3)
    ret[1] = evaluate(1)
    arrive(3)
    back = jnp.concatenate([ret[0], ret[1], ret[2]], axis=1)
    found = dot(split3(back), sel[...])
    mean = found[0:1] + found[8:9] + found[16:17]
    nb[...] = 0.5 * bias[...].astype(F32) - 2.0 * (mean - thresh[0])

    for kind in range(4):
        @pl.when(has_left)
        def _():
            pairs[kind][0].wait_send()

        @pl.when(has_right)
        def _():
            pairs[kind][1].wait_send()
    store.wait()


def shards(mask, kernel_spectra, kernel_weights, threshold, eval_tile, site_coords, bias_steps):
    rows, cols = mask.shape
    row_freqs, kernels, col_freqs = kernel_spectra.shape[1:]
    frags = eval_tile.shape[0]
    cap = frags // 2
    made = [jnp.asarray(x) for x in tables(rows, cols, row_freqs, col_freqs)]
    vmem = pl.BlockSpec(memory_space=pltpu.VMEM)
    smem = pl.BlockSpec(memory_space=pltpu.SMEM)
    anywhere = pl.BlockSpec(memory_space=pl.ANY)
    coarse = cols // GRID_STEP
    resist, new_bias = pl.pallas_call(
        kernel,
        out_shape=(jax.ShapeDtypeStruct((rows, cols), F32), jax.ShapeDtypeStruct((1, frags), F32)),
        in_specs=[vmem, anywhere, smem, smem, vmem, vmem, vmem] + [vmem] * 6 + [anywhere] * 2,
        out_specs=(anywhere, vmem),
        scratch_shapes=[
            pltpu.VMEM((rows + 2 * HALO, 2 * col_freqs), BF),
            pltpu.VMEM((3, 2 * SITES, cap), F32),
            pltpu.VMEM((3, 2 * SITES, cap), F32),
            pltpu.VMEM((rows, coarse), BF),
            pltpu.VMEM((2, REACH, coarse), F32),
            pltpu.VMEM((2, REACH, coarse), F32),
            pltpu.VMEM((3, 8, cap), F32),
            pltpu.VMEM((3, 8, cap), F32),
            pltpu.VMEM((3 * cap, frags), BF),
            pltpu.VMEM(kernel_spectra.shape, F32),
            pltpu.VMEM((2 * coarse, cols), BF),
            pltpu.VMEM((cols, coarse), BF),
            pltpu.VMEM((rows, cols), F32),
            pltpu.VMEM((cols, rows), BF),
            pltpu.SemaphoreType.DMA((4,)),
            pltpu.SemaphoreType.DMA((4, 2)),
            pltpu.SemaphoreType.DMA((4, 2)),
        ],
        compiler_params=pltpu.CompilerParams(
            collective_id=0, has_side_effects=True, vmem_limit_bytes=48 << 20),
    )(mask, kernel_spectra, kernel_weights, threshold, eval_tile.reshape(1, frags), site_coords,
      bias_steps.reshape(1, frags), *made)
    return resist, new_bias.reshape(frags)


def solution(mesh):
    placed = (
        P(("groups", "tx"), None),
        P(),
        P(),
        P(),
        P(("groups", "tx")),
        P(None, None, ("groups", "tx")),
        P(("groups", "tx")),
    )
    return jax.shard_map(
        shards,
        mesh=mesh,
        in_specs=placed,
        out_specs=(P(("groups", "tx"), None), P(("groups", "tx"))),
        check_vma=False,
    )
```

time: 176 us -> 39 us (0.22)
  the two profiles are of different devices: /device:TPU:24 before, /device:TPU:1 now
where the time goes in v1:
time: 39 us; the launch traced here: 38.6 us
  Pallas kernels  27.8 us (71%)
  local copies, waits for them, and re-layouts  9.26 us (24%)
  between operations  1.56 us (4%)
    pallas_call x1, Pallas kernels, shards(): pl.pallas_call(kernel, out_shape=(jax.ShapeDtypeStruct((rows, cols), F32)...  27.8 us
    unnamed x29, local copies, waits for them, and re-layouts  9.26 us

profile of v1, /device:TPU:1, one launch (start us, length us, event | category | flops | bytes accessed | tf_op | source)
XLA Modules:
  0.0 38.6 jit_solution(9978790318204970342)
XLA Ops:
  0.6 0.0 copy-start.2
  0.6 0.0 copy-start
  0.7 0.0 copy-start.7
  0.7 0.0 copy-start.3
  0.7 0.0 copy-start.11
  0.7 0.0 copy-start.10
  0.7 0.0 copy-start.12
  0.7 0.0 copy-start.1
  1.5 3.1 %copy.17.spectra = f32[2,96,12,128]{3,2,1,0:T(8,128)} copy(f32[2,96,12,128]{3,1,2,0:T(8,128)} %param.16) | data formatting | bytes 2359296 | tf_op args[1]
  4.6 0.0 copy-done.2
  4.6 0.0 copy-done
  4.6 0.0 copy-done.7
  4.7 0.0 copy-done.3
  4.7 0.0 copy-done.11
  4.7 0.0 copy-done.10
  4.7 0.0 copy-done.12
  4.7 0.0 copy-done.1
  4.7 0.0 copy-start.4
  4.7 1.0 %copy-done.4 = bf16[192,768]{1,0:T(8,128)(2,1)S(1)} copy-done((bf16[192,768]{1,0:T(8,128)(2,1)S(1)}, bf16[192,768]{1,0:T(8,128)(2,1)}, u32[]{:S(2)}) %copy-start.4) | copy-done | bytes 294936
  5.7 0.0 copy-start.5
  5.7 0.9 %copy-done.5 = bf16[256,512]{1,0:T(8,128)(2,1)S(1)} copy-done((bf16[256,512]{1,0:T(8,128)(2,1)S(1)}, bf16[256,512]{1,0:T(8,128)(2,1)}, u32[]{:S(2)}) %copy-start.5) | copy-done | bytes 262168
  6.6 0.0 copy-start.6
  6.6 0.9 %copy-done.6 = bf16[512,192]{1,0:T(8,128)(2,1)S(1)} copy-done((bf16[512,192]{1,0:T(8,128)(2,1)S(1)}, bf16[512,192]{1,0:T(8,128)(2,1)}, u32[]{:S(2)}) %copy-start.6) | copy-done | bytes 196632
  7.6 0.0 copy-start.8
  7.6 0.8 %copy-done.8 = f32[2,16,512]{2,1,0:T(8,128)S(1)} copy-done((f32[2,16,512]{2,1,0:T(8,128)S(1)}, f32[2,16,512]{2,1,0:T(8,128)}, u32[]{:S(2)}) %copy-start.8) | copy-done | bytes 65560
  8.4 0.0 copy-start.9
  8.4 0.8 %copy-done.9 = bf16[256,16]{1,0:T(8,128)(2,1)S(1)} copy-done((bf16[256,16]{1,0:T(8,128)(2,1)S(1)}, bf16[256,16]{1,0:T(8,128)(2,1)}, u32[]{:S(2)}) %copy-start.9) | copy-done | bytes 8216
  9.3 27.8 %shard_map.158 = (f32[256,1024]{1,0:T(8,128)S(1)}, f32[1,512]{1,0:T(1,128)S(1)}) custom-call(bf16[256,1024]{1,0:T(8,128)(2,1)S(1)} %copy-done.1, f32[2,96,12,128]{3,2,1,0:T(8,128)} %copy.17.spectra, f32[12]{0:T(128)S(1)} %copy-done.12, f32[1]{0:T(128)S(6)} %copy.20.thresh, s32[1,512]{1,0:T(1,128)S(1)} %bitcast.3, f32[2,16,512]{2,1,0:T(8,128)S(1)} %copy-done.8, ...), custom_call_target="tpu_custom_call" | custom-call | tf_op jit(solution)/shard_map/pallas_call | solution.py:318
  37.1 1.0 %copy.21 = f32[256,1024]{1,0:T(8,128)} copy(f32[256,1024]{1,0:T(8,128)S(1)} %get-tuple-element.8) | data formatting | bytes 2097152
  38.1 0.6 %copy.22 = f32[512]{0:T(512)} copy(f32[512]{0:T(512)S(1)} %bitcast.5) | data formatting | bytes 4096
Async XLA Ops:
  0.6 4.0 %copy-start.2 = (bf16[1024,256]{1,0:T(8,128)(2,1)S(1)}, bf16[1024,256]{1,0:T(8,128)(2,1)}, u32[]{:S(2)}) copy-start(bf16[1024,256]{1,0:T(8,128)(2,1)} %constant.23.clone.wide_t_h) | copy-start | bytes 1572868
  0.6 4.0 %copy-start = (bf16[512,1024]{1,0:T(8,128)(2,1)S(1)}, bf16[512,1024]{1,0:T(8,128)(2,1)}, u32[]{:S(2)}) copy-start(bf16[512,1024]{1,0:T(8,128)(2,1)} %constant.22.clone.wide_h) | copy-start | bytes 3145732
  0.7 4.0 %copy-start.7 = (bf16[256,256]{1,0:T(8,128)(2,1)S(1)}, bf16[256,256]{1,0:T(8,128)(2,1)}, u32[]{:S(2)}) copy-start(bf16[256,256]{1,0:T(8,128)(2,1)} %constant.20.clone.rmid) | copy-start | bytes 393220
  0.7 4.0 %copy-start.3 = (bf16[1024,256]{1,0:T(8,128)(2,1)S(1)}, bf16[1024,256]{1,0:T(8,128)(2,1)}, u32[]{:S(2)}) copy-start(bf16[1024,256]{1,0:T(8,128)(2,1)} %constant.16.clone.colf) | copy-start | bytes 1572868
  0.7 4.0 %copy-start.11 = (s32[512]{0:T(512)S(1)}, s32[512]{0:T(512)}, u32[]{:S(2)}) copy-start(s32[512]{0:T(512)} %param.21) | copy-start | bytes 6148
  0.7 4.0 %copy-start.10 = (s32[512]{0:T(512)S(1)}, s32[512]{0:T(512)}, u32[]{:S(2)}) copy-start(s32[512]{0:T(512)} %param.19) | copy-start | bytes 6148
  0.7 4.0 %copy-start.12 = (f32[12]{0:T(128)S(1)}, f32[12]{0:T(128)}, u32[]{:S(2)}) copy-start(f32[12]{0:T(128)} %weights.1) | copy-start | bytes 148
  0.7 4.0 %copy-start.1 = (bf16[256,1024]{1,0:T(8,128)(2,1)S(1)}, bf16[256,1024]{1,0:T(8,128)(2,1)}, u32[]{:S(2)}) copy-start(bf16[256,1024]{1,0:T(8,128)(2,1)} %mask.1) | copy-start | bytes 1572868
  4.7 1.0 %copy-start.4 = (bf16[192,768]{1,0:T(8,128)(2,1)S(1)}, bf16[192,768]{1,0:T(8,128)(2,1)}, u32[]{:S(2)}) copy-start(bf16[192,768]{1,0:T(8,128)(2,1)} %constant.17.clone.rowf) | copy-start | bytes 884740
  5.7 0.9 %copy-start.5 = (bf16[256,512]{1,0:T(8,128)(2,1)S(1)}, bf16[256,512]{1,0:T(8,128)(2,1)}, u32[]{:S(2)}) copy-start(bf16[256,512]{1,0:T(8,128)(2,1)} %constant.19.clone.cinv) | copy-start | bytes 786436
  6.6 0.9 %copy-start.6 = (bf16[512,192]{1,0:T(8,128)(2,1)S(1)}, bf16[512,192]{1,0:T(8,128)(2,1)}, u32[]{:S(2)}) copy-start(bf16[512,192]{1,0:T(8,128)(2,1)} %constant.18.clone.rinv) | copy-start | bytes 589828
  7.6 0.8 %copy-start.8 = (f32[2,16,512]{2,1,0:T(8,128)S(1)}, f32[2,16,512]{2,1,0:T(8,128)}, u32[]{:S(2)}) copy-start(f32[2,16,512]{2,1,0:T(8,128)} %sc.1) | copy-start | bytes 196612
  8.4 0.8 %copy-start.9 = (bf16[256,16]{1,0:T(8,128)(2,1)S(1)}, bf16[256,16]{1,0:T(8,128)(2,1)}, u32[]{:S(2)}) copy-start(bf16[256,16]{1,0:T(8,128)(2,1)} %constant.21.clone.redge) | copy-start | bytes 24580

commit v2 on v1

--- a/solution.py
+++ b/solution.py
@@ -18,6 +18,7 @@
 BF = jnp.bfloat16
 F32 = jnp.float32
 MESH = pl.DeviceIdType.MESH
+LOADED = ("mask", "colf", "ev", "sc", "rowf", "ks", "rinv", "cinv", "rmid", "redge", "wide_t", "wide")
 
 
 def host_bf16(x):
@@ -95,16 +96,20 @@
     return jnp.maximum(1.0 - jnp.abs(distance), 0.0)
 
 
-def kernel(mask, spectra, weights, thresh, ev, sc, bias, colf, rowf, rinv, cinv, rmid, redge,
-           wide_h, wide_t_h, resist_h, nb,
-           win, snd, recs, inten, hsnd, halo, rsnd, ret, sel, ksv, wide, wide_t, resist, rt,
-           local_sem, send_sem, recv_sem):
+def kernel(weights_h, *refs):
+    n = len(LOADED)
+    sources = dict(zip(LOADED, refs[:n]))
+    resist_h, mean_out = refs[n:n + 2]
+    held = dict(zip(LOADED, refs[n + 2:2 * n + 2]))
+    (weights, win, snd, recs, inten, hsnd, halo, rsnd, ret, sel, resist, rt,
+     local_sem, send_sem, recv_sem) = refs[2 * n + 2:]
+    mask, colf, ev, sc, rowf, ksv, rinv, cinv, rmid, redge, wide_t, wide = (held[k] for k in LOADED)
     t = lax.axis_index("tx")
     count = lax.axis_size("tx")
     has_left = t > 0
     has_right = t < count - 1
     rows, cols = mask.shape
-    row_freqs, kernels, col_freqs = ksv.shape[1:]
+    kernels, row_freqs, col_freqs = ksv.shape[1:]
     frags = ev.shape[1]
     cap = frags // 2
 
@@ -118,12 +123,12 @@
     def _():
         pl.semaphore_signal(barrier, inc=1, device_id={"tx": t + 1}, device_id_type=MESH)
 
-    load_ks = pltpu.make_async_copy(spectra, ksv, local_sem.at[0])
-    load_wide = pltpu.make_async_copy(wide_h, wide, local_sem.at[1])
-    load_wide_t = pltpu.make_async_copy(wide_t_h, wide_t, local_sem.at[2])
-    load_ks.start()
-    load_wide.start()
-    load_wide_t.start()
+    loads = {k: pltpu.make_async_copy(sources[k], held[k], local_sem.at[i])
+             for i, k in enumerate(LOADED)}
+    for k in LOADED:
+        loads[k].start()
+    load_weights = pltpu.make_async_copy(weights_h, weights, local_sem.at[n])
+    load_weights.start()
 
     def to_left(kind, src, dst):
         return pltpu.make_async_remote_copy(
@@ -175,6 +180,8 @@
         halo[1] = jnp.zeros(halo.shape[1:], F32)
         ret[2] = jnp.zeros(ret.shape[1:], F32)
 
+    loads["mask"].wait()
+    loads["colf"].wait()
     win[HALO:HALO + rows] = dot(mask[...], colf[...]).astype(BF)
 
     between = jnp.logical_and(has_left, has_right)
@@ -189,6 +196,8 @@
 
     start(0)
 
+    loads["ev"].wait()
+    loads["sc"].wait()
     offset = ev[...] - t + 1
     member = jnp.where(lax.broadcasted_iota(jnp.int32, (8, frags), 0) == offset, 1.0, 0.0)
     upper = jnp.where(
@@ -208,8 +217,11 @@
     snd[2] = packed[:, 2 * cap:]
     start(1)
 
+    loads["rowf"].wait()
     product = dot(rowf[:, HALO:HALO + rows], win[HALO:HALO + rows])
-    load_ks.wait()
+    for k in ("ks", "rinv", "cinv", "rmid", "redge"):
+        loads[k].wait()
+    load_weights.wait()
     arrive(0)
     product = product + dot(rowf[:, :HALO], win[:HALO]) + dot(rowf[:, HALO + rows:], win[HALO + rows:])
     real = product[:row_freqs, :col_freqs] - product[row_freqs:, col_freqs:]
@@ -220,8 +232,8 @@
     for pair in range(kernels // 2):
         blocks = []
         for k in (2 * pair, 2 * pair + 1):
-            kr = ksv[0, :, k, :]
-            ki = ksv[1, :, k, :]
+            kr = ksv[0, k]
+            ki = ksv[1, k]
             blocks.append(jnp.concatenate(
                 [(kr * real - ki * imag).astype(BF), (kr * imag + ki * real).astype(BF)], axis=0))
         field = dot(rinv[...], jnp.concatenate(blocks, axis=1)).astype(BF)
@@ -244,12 +256,12 @@
     center = jnp.sum(blurred) * (1.0 / (blurred.shape[0] * blurred.shape[1]))
     high = blurred.astype(BF)
     low = (blurred - high.astype(F32)).astype(BF)
-    load_wide_t.wait()
+    loads["wide_t"].wait()
     rt[...] = (dot_nt(wide_t[...], high) + dot_nt(wide_t[...], low) - center).astype(BF)
-    load_wide.wait()
+    loads["wide"].wait()
     coarse = high.shape[1]
     resist[...] = (dot(high, wide[:coarse]) + dot(low, wide[:coarse])) + dot(high, wide[coarse:])
-    store = pltpu.make_async_copy(resist, resist_h, local_sem.at[3])
+    store = pltpu.make_async_copy(resist, resist_h, local_sem.at[n + 1])
     store.start()
     arrive(1)
 
@@ -291,8 +303,7 @@
     arrive(3)
     back = jnp.concatenate([ret[0], ret[1], ret[2]], axis=1)
     found = dot(split3(back), sel[...])
-    mean = found[0:1] + found[8:9] + found[16:17]
-    nb[...] = 0.5 * bias[...].astype(F32) - 2.0 * (mean - thresh[0])
+    mean_out[...] = (found[0:1] + found[8:9] + found[16:17]).reshape(frags)
 
     for kind in range(4):
         @pl.when(has_left)
@@ -310,17 +321,23 @@
     row_freqs, kernels, col_freqs = kernel_spectra.shape[1:]
     frags = eval_tile.shape[0]
     cap = frags // 2
-    made = [jnp.asarray(x) for x in tables(rows, cols, row_freqs, col_freqs)]
+    names = ("colf", "rowf", "rinv", "cinv", "rmid", "redge", "wide", "wide_t")
+    values = dict(zip(names, (jnp.asarray(x) for x in tables(rows, cols, row_freqs, col_freqs))))
+    values["mask"] = mask
+    values["ks"] = jnp.transpose(kernel_spectra, (0, 2, 1, 3))
+    values["ev"] = eval_tile.reshape(1, frags)
+    values["sc"] = site_coords
+    ordered = [values[k] for k in LOADED]
     vmem = pl.BlockSpec(memory_space=pltpu.VMEM)
-    smem = pl.BlockSpec(memory_space=pltpu.SMEM)
-    anywhere = pl.BlockSpec(memory_space=pl.ANY)
+    hbm = pl.BlockSpec(memory_space=pltpu.HBM)
     coarse = cols // GRID_STEP
-    resist, new_bias = pl.pallas_call(
+    resist, mean = pl.pallas_call(
         kernel,
-        out_shape=(jax.ShapeDtypeStruct((rows, cols), F32), jax.ShapeDtypeStruct((1, frags), F32)),
-        in_specs=[vmem, anywhere, smem, smem, vmem, vmem, vmem] + [vmem] * 6 + [anywhere] * 2,
-        out_specs=(anywhere, vmem),
-        scratch_shapes=[
+        out_shape=(jax.ShapeDtypeStruct((rows, cols), F32), jax.ShapeDtypeStruct((frags,), F32)),
+        in_specs=[hbm] * (1 + len(ordered)),
+        out_specs=(pl.BlockSpec(memory_space=pl.ANY), vmem),
+        scratch_shapes=[pltpu.VMEM(x.shape, x.dtype) for x in ordered] + [
+            pltpu.SMEM((kernels,), F32),
             pltpu.VMEM((rows + 2 * HALO, 2 * col_freqs), BF),
             pltpu.VMEM((3, 2 * SITES, cap), F32),
             pltpu.VMEM((3, 2 * SITES, cap), F32),
@@ -330,20 +347,17 @@
             pltpu.VMEM((3, 8, cap), F32),
             pltpu.VMEM((3, 8, cap), F32),
             pltpu.VMEM((3 * cap, frags), BF),
-            pltpu.VMEM(kernel_spectra.shape, F32),
-            pltpu.VMEM((2 * coarse, cols), BF),
-            pltpu.VMEM((cols, coarse), BF),
             pltpu.VMEM((rows, cols), F32),
             pltpu.VMEM((cols, rows), BF),
-            pltpu.SemaphoreType.DMA((4,)),
+            pltpu.SemaphoreType.DMA((len(ordered) + 2,)),
             pltpu.SemaphoreType.DMA((4, 2)),
             pltpu.SemaphoreType.DMA((4, 2)),
         ],
         compiler_params=pltpu.CompilerParams(
-            collective_id=0, has_side_effects=True, vmem_limit_bytes=48 << 20),
-    )(mask, kernel_spectra, kernel_weights, threshold, eval_tile.reshape(1, frags), site_coords,
-      bias_steps.reshape(1, frags), *made)
-    return resist, new_bias.reshape(frags)
+            collective_id=0, has_side_effects=True, vmem_limit_bytes=63 << 20),
+    )(kernel_weights, *ordered)
+    new_bias = 0.5 * bias_steps.astype(F32) - 2.0 * (mean - threshold[0])
+    return resist, new_bias
 
 
 def solution(mesh):

time: 39 us -> 31.1 us (0.80)
  local copies, waits for them, and re-layouts: 9.26 us -> 2.31 us
  Pallas kernels: 27.8 us -> 25.9 us
  other arithmetic: 0 us -> 1.24 us
    unnamed x29 -> x3, local copies, waits for them, and re-layouts: 9.26 us -> 2.31 us
    pallas_call x1, Pallas kernels: 27.8 us -> 25.9 us  [shards(): pl.pallas_call(kernel, out_shape=(jax.ShapeDtypeStruct((rows, cols), F32)...]
    sub x0 -> x1, other arithmetic: none -> 1.24 us  [shards(): new_bias = 0.5 * bias_steps.astype(F32) - 2.0 * (mean - threshold[0])]
where the time goes in v2:
time: 31.1 us; the launch traced here: 30.7 us
  Pallas kernels  25.9 us (83%)
  local copies, waits for them, and re-layouts  2.31 us (7%)
  between operations  1.3 us (4%)
  other arithmetic  1.24 us (4%)
    pallas_call x1, Pallas kernels, shards(): pl.pallas_call(kernel, out_shape=(jax.ShapeDtypeStruct((rows, cols), F32)...  25.9 us
    unnamed x3, local copies, waits for them, and re-layouts  2.31 us
    sub x1, other arithmetic, shards(): new_bias = 0.5 * bias_steps.astype(F32) - 2.0 * (mean - threshold[0])  1.24 us

profile of v2, /device:TPU:1, one launch (start us, length us, event | category | flops | bytes accessed | tf_op | source)
XLA Modules:
  0.0 30.7 jit_solution(17621244352763946158)
XLA Ops:
  0.6 0.0 copy-start
  0.6 25.9 %shard_map.158 = (f32[256,1024]{1,0:T(8,128)}, f32[512]{0:T(512)}) custom-call(f32[12]{0:T(128)} %weights_h.1, bf16[256,1024]{1,0:T(8,128)(2,1)} %refs_0_.1, bf16[1024,256]{1,0:T(8,128)(2,1)} %constant.20.clone.refs_1_, s32[1,512]{1,0:T(1,128)} %bitcast.5, f32[2,16,512]{2,1,0:T(8,128)} %refs_3_.1, bf16[192,768]{1,0:T(8,128)(2,1)} %constant.21.clone.refs_4_, ...), custom_call_target="tpu_custom_call" | custom-call | tf_op jit(solution)/shard_map/pallas_call | solution.py:334
  27.2 0.0 copy-done
  27.2 1.2 %multiply_subtract_fusion = f32[512]{0:T(512)} fusion(f32[512]{0:T(512)} %get-tuple-element.5, s32[512]{0:T(512)S(1)} %copy-done, f32[]{:T(128)} %bitcast.3), kind=kLoop, calls=%fused_computation | loop fusion | flops 2560 | bytes 6148 | tf_op jit(solution)/shard_map/sub | solution.py:359
  28.4 2.3 %copy.19 = f32[256,1024]{1,0:T(8,128)} copy(f32[256,1024]{1,0:T(8,128)} %get-tuple-element.8) | data formatting | bytes 2097152
Async XLA Ops:
  0.6 26.5 %copy-start = (s32[512]{0:T(512)S(1)}, s32[512]{0:T(512)}, u32[]{:S(2)}) copy-start(s32[512]{0:T(512)} %param.21) | copy-start | bytes 6148

commit v3 on v2

--- a/solution.py
+++ b/solution.py
@@ -18,7 +18,7 @@
 BF = jnp.bfloat16
 F32 = jnp.float32
 MESH = pl.DeviceIdType.MESH
-LOADED = ("mask", "colf", "ev", "sc", "rowf", "ks", "rinv", "cinv", "rmid", "redge", "wide_t", "wide")
+LOADED = ("mask", "colf", "ev", "sc", "rowf", "ks", "rinv", "cinv", "rmid", "redge", "wide_t")
 
 
 def host_bf16(x):
@@ -99,16 +99,17 @@
 def kernel(weights_h, *refs):
     n = len(LOADED)
     sources = dict(zip(LOADED, refs[:n]))
-    resist_h, mean_out = refs[n:n + 2]
+    tile_h, mean_out = refs[n:n + 2]
     held = dict(zip(LOADED, refs[n + 2:2 * n + 2]))
-    (weights, win, snd, recs, inten, hsnd, halo, rsnd, ret, sel, resist, rt,
+    (weights, win, snd, recs, inten, hsnd, halo, rsnd, ret, sel, tile, rt,
      local_sem, send_sem, recv_sem) = refs[2 * n + 2:]
-    mask, colf, ev, sc, rowf, ksv, rinv, cinv, rmid, redge, wide_t, wide = (held[k] for k in LOADED)
+    mask, colf, ev, sc, rowf, ksv, rinv, cinv, rmid, redge, wide_t = (held[k] for k in LOADED)
     t = lax.axis_index("tx")
     count = lax.axis_size("tx")
     has_left = t > 0
     has_right = t < count - 1
     rows, cols = mask.shape
+    coarse = cols // GRID_STEP
     kernels, row_freqs, col_freqs = ksv.shape[1:]
     frags = ev.shape[1]
     cap = frags // 2
@@ -258,10 +259,9 @@
     low = (blurred - high.astype(F32)).astype(BF)
     loads["wide_t"].wait()
     rt[...] = (dot_nt(wide_t[...], high) + dot_nt(wide_t[...], low) - center).astype(BF)
-    loads["wide"].wait()
-    coarse = high.shape[1]
-    resist[...] = (dot(high, wide[:coarse]) + dot(low, wide[:coarse])) + dot(high, wide[coarse:])
-    store = pltpu.make_async_copy(resist, resist_h, local_sem.at[n + 1])
+    tile[:, :coarse] = high
+    tile[:, coarse:] = low
+    store = pltpu.make_async_copy(tile, tile_h, local_sem.at[n + 1])
     store.start()
     arrive(1)
 
@@ -290,9 +290,11 @@
             return acc + after * hat(end_line - local)
 
         def step(i, acc):
-            return one(2 * i + 1, one(2 * i, acc))
-
-        acc = lax.fori_loop(0, SITES // 2, step, jnp.zeros((8, cap), F32))
+            for j in range(8):
+                acc = one(8 * i + j, acc)
+            return acc
+
+        acc = lax.fori_loop(0, SITES // 8, step, jnp.zeros((8, cap), F32))
         mean = jnp.sum(acc, axis=0, keepdims=True) * (1.0 / SITES) + center
         return jnp.broadcast_to(mean, (8, cap))
 
@@ -314,6 +316,18 @@
         def _():
             pairs[kind][1].wait_send()
     store.wait()
+
+
+def finish(tile, wide, mean, bias, thresh, resist, nb):
+    coarse = wide.shape[0] // 2
+    high = tile[:, :coarse]
+    low = tile[:, coarse:]
+    upper = wide[:coarse]
+    resist[...] = (dot(high, upper) + dot(low, upper)) + dot(high, wide[coarse:])
+
+    @pl.when(pl.program_id(0) == 0)
+    def _():
+        nb[...] = 0.5 * bias[...].astype(F32) - 2.0 * (mean[...] - thresh[0])
 
 
 def shards(mask, kernel_spectra, kernel_weights, threshold, eval_tile, site_coords, bias_steps):
@@ -331,9 +345,9 @@
     vmem = pl.BlockSpec(memory_space=pltpu.VMEM)
     hbm = pl.BlockSpec(memory_space=pltpu.HBM)
     coarse = cols // GRID_STEP
-    resist, mean = pl.pallas_call(
+    tile, mean = pl.pallas_call(
         kernel,
-        out_shape=(jax.ShapeDtypeStruct((rows, cols), F32), jax.ShapeDtypeStruct((frags,), F32)),
+        out_shape=(jax.ShapeDtypeStruct((rows, 2 * coarse), BF), jax.ShapeDtypeStruct((frags,), F32)),
         in_specs=[hbm] * (1 + len(ordered)),
         out_specs=(pl.BlockSpec(memory_space=pl.ANY), vmem),
         scratch_shapes=[pltpu.VMEM(x.shape, x.dtype) for x in ordered] + [
@@ -347,7 +361,7 @@
             pltpu.VMEM((3, 8, cap), F32),
             pltpu.VMEM((3, 8, cap), F32),
             pltpu.VMEM((3 * cap, frags), BF),
-            pltpu.VMEM((rows, cols), F32),
+            pltpu.VMEM((rows, 2 * coarse), BF),
             pltpu.VMEM((cols, rows), BF),
             pltpu.SemaphoreType.DMA((len(ordered) + 2,)),
             pltpu.SemaphoreType.DMA((4, 2)),
@@ -356,7 +370,21 @@
         compiler_params=pltpu.CompilerParams(
             collective_id=0, has_side_effects=True, vmem_limit_bytes=63 << 20),
     )(kernel_weights, *ordered)
-    new_bias = 0.5 * bias_steps.astype(F32) - 2.0 * (mean - threshold[0])
+    parts = 2
+    whole = lambda i: (0,)
+    resist, new_bias = pl.pallas_call(
+        finish,
+        grid=(parts,),
+        out_shape=(jax.ShapeDtypeStruct((rows, cols), F32), jax.ShapeDtypeStruct((frags,), F32)),
+        in_specs=[
+            pl.BlockSpec((rows, 2 * coarse), lambda i: (0, 0)),
+            pl.BlockSpec((2 * coarse, cols // parts), lambda i: (0, i)),
+            pl.BlockSpec((frags,), whole),
+            pl.BlockSpec((frags,), whole),
+            pl.BlockSpec(memory_space=pltpu.SMEM),
+        ],
+        out_specs=(pl.BlockSpec((rows, cols // parts), lambda i: (0, i)), pl.BlockSpec((frags,), whole)),
+    )(tile, values["wide"], mean, bias_steps, threshold)
     return resist, new_bias
 
 

time: 31.1 us -> 25.4 us (0.82)
  local copies, waits for them, and re-layouts: 2.31 us -> 0 us
  Pallas kernels: 25.9 us -> 23.8 us
  other arithmetic: 1.24 us -> 0 us
    unnamed x3 -> x0, local copies, waits for them, and re-layouts: 2.31 us -> none
    pallas_call x1 -> x2, Pallas kernels: 25.9 us -> 23.8 us  [the longest x1 21.1 us: shards(): pl.pallas_call(kernel, out_shape=(jax.ShapeDtypeStruct((rows, 2 * coarse)...]
    sub x1 -> x0, other arithmetic: 1.24 us -> none  [shards(): new_bias = 0.5 * bias_steps.astype(F32) - 2.0 * (mean - threshold[0])]
where the time goes in v3:
time: 25.4 us; the launch traced here: 25.1 us
  Pallas kernels  23.8 us (94%)
  between operations  1.29 us (5%)
    pallas_call x1, Pallas kernels, shards(): pl.pallas_call(kernel, out_shape=(jax.ShapeDtypeStruct((rows, 2 * coarse)...  21.1 us
    pallas_call x1, Pallas kernels, shards(): pl.pallas_call(finish, grid=(parts,), out_shape=(jax.ShapeDtypeStruct((ro...  2.7 us

profile of v3, /device:TPU:1, one launch (start us, length us, event | category | flops | bytes accessed | tf_op | source)
XLA Modules:
  0.0 25.1 jit_solution(4248127498290060225)
XLA Ops:
  1.3 21.1 %shard_map.158 = (bf16[256,512]{1,0:T(8,128)(2,1)}, f32[512]{0:T(512)}) custom-call(f32[12]{0:T(128)} %weights_h.1, bf16[256,1024]{1,0:T(8,128)(2,1)} %refs_0_.1, bf16[1024,256]{1,0:T(8,128)(2,1)} %constant.16.clone.refs_1_, s32[1,512]{1,0:T(1,128)} %bitcast.3, f32[2,16,512]{2,1,0:T(8,128)} %refs_3_.1, bf16[192,768]{1,0:T(8,128)(2,1)} %constant.17.clone.refs_4_, ...), custom_call_target="tpu_custom_call" | custom-call | tf_op jit(solution)/shard_map/pallas_call | solution.py:348
  22.4 2.7 %shard_map.159 = (f32[256,1024]{1,0:T(8,128)}, f32[512]{0:T(512)}) custom-call(bf16[256,512]{1,0:T(8,128)(2,1)} %get-tuple-element.4.tile, bf16[512,1024]{1,0:T(8,128)(2,1)} %constant.22.clone.wide, f32[512]{0:T(512)} %get-tuple-element.5.mean, s32[512]{0:T(512)} %bias.1, f32[1]{0:T(128)S(6)} %copy.17.thresh), custom_call_target="tpu_custom_call" | custom-call | tf_op jit(solution)/shard_map/pallas_call | solution.py:375
